TPU v7x, 32 devices: a whole 2x2x4 slice. The times are simulated.
32 devices in a mesh: prow: 2 (over y), pcol: 16 (over z, x, core).
Axes of the slice: x: 2, y: 2, z: 4, core: 2. Of those that a mesh axis runs over, the one named last changes fastest.
Arguments:
- ancestor_inverse: bfloat16 [24576, 24576], P('prow', 'pcol'), may hold values from -6 to 6
- tile_pattern: int32 [64, 64], replicated, may hold values 0 or 1
- rows_first: int32 [24576], replicated, may hold values 0 or 1
- rows_second: int32 [24576], replicated, may hold values 0 or 1
- panel_first: bfloat16 [24576, 512], P('prow', 'pcol'), may hold values from -0.0390625 to 0.0390625
- panel_second: bfloat16 [24576, 512], P('prow', 'pcol'), may hold values from -0.15625 to 0.15625
- inner_panel: bfloat16 [512, 512], replicated, may hold values from -0.25 to 0.25
- pivot_first: float32 [512, 512], replicated, may hold values from -6 to 6
- pivot_second: float32 [512, 512], replicated, may hold values from -6 to 6
Outputs:
- column_first: bfloat16 [24576, 512], P(('prow', 'pcol'))
- diagonal_first: float32 [512, 512], replicated
- inner_second: float32 [512, 512], replicated
- column_second: bfloat16 [24576, 512], P(('prow', 'pcol'))
- diagonal_second: float32 [512, 512], replicated
Inputs may be any that keep to these rules, and one draw needn't show every extreme that they name: `tile_pattern`: 1 marks a structurally nonzero tile. `rows_first`: 1 marks a row of the first supernode's structure. By construction here, a row belongs to the second supernode's structure only where both rows_second and rows_first are 1.
All inputs are finite; a program needn't handle non-finite values.
Results may differ from a plain program's by a relative error of at most 0.015.
Values may be sent and summed in bfloat16 or wider, within the bound.
No kernel may reach another device: no remote copies, remote signals or barrier semaphores. Data moves between devices by JAX's collectives and lax.ppermute only.
A program may use at most 256 MiB of HBM per device.

v0:
```python
import jax
import jax.numpy as jnp
from jax import lax
from jax.sharding import PartitionSpec as P

TILE = 384


def from_root(shard, axis, root):
    mine = lax.axis_index(axis) == root
    return lax.psum(jnp.where(mine, shard, jnp.zeros_like(shard)), axis)


def mask_tiles(block, pattern, row_start, col_start):
    tile_rows = block.shape[0] // TILE
    tile_cols = block.shape[1] // TILE
    window = lax.dynamic_slice(pattern, (row_start, col_start), (tile_rows, tile_cols)).astype(
        jnp.bfloat16
    )
    shaped = block.reshape(tile_rows, TILE, tile_cols, TILE) * window[:, None, :, None]
    return shaped.reshape(block.shape)


def body(
    ancestor_inverse,
    tile_pattern,
    rows_first,
    rows_second,
    panel_first,
    panel_second,
    inner_panel,
    pivot_first,
    pivot_second,
):
    row_count = lax.axis_size("prow")
    col_count = lax.axis_size("pcol")
    row_id = lax.axis_index("prow")
    col_id = lax.axis_index("pcol")
    row_block = ancestor_inverse.shape[0]
    col_block = ancestor_inverse.shape[1]
    share = row_block // col_count
    width = inner_panel.shape[0]
    sparse = mask_tiles(
        ancestor_inverse, tile_pattern, row_id * (row_block // TILE), col_id * (col_block // TILE)
    )
    struct_first = lax.dynamic_slice_in_dim(rows_first, row_id * row_block, row_block).astype(
        jnp.bfloat16
    )
    struct_second = struct_first * lax.dynamic_slice_in_dim(
        rows_second, row_id * row_block, row_block
    ).astype(jnp.bfloat16)
    local_first = panel_first * struct_first[:, None]
    local_second = panel_second * struct_second[:, None]
    source = col_id * row_count // col_count
    offset = col_id * col_block - source * row_block
    full_first, full_second = (
        lax.all_gather(local_first, "pcol", axis=1, tiled=True),
        lax.all_gather(local_second, "pcol", axis=1, tiled=True),
    )
    mirrored = (
        from_root(lax.dynamic_slice_in_dim(full_first, offset, col_block, 0), "prow", source),
        from_root(lax.dynamic_slice_in_dim(full_second, offset, col_block, 0), "prow", source),
    )
    stacked = jnp.concatenate(mirrored, axis=1)
    summed = lax.psum_scatter(
        jnp.dot(sparse, stacked, preferred_element_type=jnp.float32).astype(jnp.bfloat16),
        "pcol",
        scatter_dimension=0,
        tiled=True,
    ).astype(jnp.float32)
    sum_first = summed[:, :width]
    sum_second = summed[:, width:]
    column_first = (-sum_first).astype(jnp.bfloat16)
    own_first = lax.dynamic_slice_in_dim(full_first, col_id * share, share, 0)
    own_second = lax.dynamic_slice_in_dim(full_second, col_id * share, share, 0)
    corr_first, crossed = lax.psum(
        (
            jnp.dot(own_first.T, column_first, preferred_element_type=jnp.float32),
            jnp.dot(column_first.T, own_second, preferred_element_type=jnp.float32),
        ),
        ("prow", "pcol"),
    )
    diagonal_first = pivot_first - corr_first
    column_second = (
        -(sum_second + jnp.dot(column_first, inner_panel, preferred_element_type=jnp.float32))
    ).astype(jnp.bfloat16)
    inner_wide = inner_panel.astype(jnp.float32)
    inner_second = -(jnp.dot(diagonal_first, inner_wide, precision=lax.Precision.HIGHEST) + crossed)
    corr_second = lax.psum(
        jnp.dot(own_second.T, column_second, preferred_element_type=jnp.float32), ("prow", "pcol")
    )
    diagonal_second = (
        pivot_second
        - jnp.dot(inner_wide.T, inner_second, precision=lax.Precision.HIGHEST)
        - corr_second
    )
    return (column_first, diagonal_first, inner_second, column_second, diagonal_second)


def solution(mesh):
    return jax.shard_map(
        body,
        mesh=mesh,
        in_specs=(
            P("prow", "pcol"),
            P(),
            P(),
            P(),
            P("prow", "pcol"),
            P("prow", "pcol"),
            P(),
            P(),
            P(),
        ),
        out_specs=(P(("prow", "pcol"), None), P(), P(), P(("prow", "pcol"), None), P()),
        check_vma=False,
    )
```

profile of v0, /device:TPU:0, one launch (start us, length us, event | category | flops | bytes accessed | tf_op | source)
XLA Modules:
  0.0 757.5 jit_solution(4436610214405602834)
XLA Ops:
  7.2 0.0 all-gather.5.cloned.1.call-start
  7.2 0.9 fusion.20
  8.1 2.1 broadcast_multiply_fusion
  10.2 0.0 all-gather.5.cloned.1.call-update
  10.2 0.0 all-gather.3.cloned.1.call-start
  10.3 2.1 broadcast_multiply_fusion.1
  12.4 0.0 all-reduce.7.cloned.1.call-start
  12.5 101.6 %all-gather.5.cloned.1.call-done = bf16[12288,512]{0,1:T(8,128)(2,1)} async-done(((bf16[12288,32]{0,1:T(8,128)(2,1)}), bf16[12288,512]{0,1:T(8,128)(2,1)}) %all-gather.5.cloned.1.call-update) | async-done | bytes 12582928 | tf_op jit(solution)/shard_map/all_gather | solution.py:58
  114.0 2.8 dynamic-slice_select_fusion
  116.9 98.7 %all-gather.3.cloned.1.call-done = bf16[12288,512]{0,1:T(8,128)(2,1)} async-done(((bf16[12288,32]{0,1:T(8,128)(2,1)}), bf16[12288,512]{0,1:T(8,128)(2,1)}) %all-gather.3.cloned.1.call-update) | async-done | bytes 12582928 | tf_op jit(solution)/shard_map/all_gather | solution.py:57
  215.6 2.8 dynamic-slice_select_fusion.1
  218.4 0.0 reduce-scatter.2.cloned.1.call-start
  218.5 0.1 dynamic-slice_convert_fusion.2
  218.6 14.1 %mul.55 = bf16[32,384,4,384]{3,2,1,0:T(4,128)(2,1)} broadcast(bf16[32,4]{1,0:T(8,128)(2,1)S(1)} %dynamic-slice_convert_fusion.2), dimensions={0,2} | broadcast | bytes 37748992 | tf_op jit(solution)/shard_map/mul | solution.py:20
  232.7 26.1 %copy.18 = bf16[1536,8,4,384]{3,1,2,0:T(8,128)(2,1)} copy(bf16[1536,8,4,384]{3,2,1,0:T(4,128)(2,1)} %bitcast.18) | data formatting | bytes 75497472
  258.8 43.9 %all-reduce.7.cloned.1.call-done = (bf16[1536,512]{0,1:T(8,128)(2,1)}, bf16[1536,512]{0,1:T(8,128)(2,1)}) async-done(((bf16[1536,512]{0,1:T(8,128)(2,1)}, bf16[1536,512]{0,1:T(8,128)(2,1)}), (bf16[1536,512]{0,1:T(8,128)(2,1)}, bf16[1536,512]{0,1:T(8,128)(2,1)})) %all-reduce.7.cloned.1.call-update) | async-done | bytes 3145744 | tf_op jit(solution)/shard_map/psum | solution.py:11
  302.7 48.0 %fusion.2 = bf16[12288,1024]{1,0:T(8,128)(2,1)} fusion(bf16[12288,1536]{1,0:T(8,128)(2,1)} %param.9, bf16[12288,1536]{1,0:T(8,128)(2,1)} %bitcast.19, bf16[1536,512]{0,1:T(8,128)(2,1)} %get-tuple-element.13, bf16[1536,512]{0,1:T(8,128)(2,1)} %get-tuple-element.14), kind=kOutput, calls=%fused_computation.2 | convolution fusion | flops 38692454400 | bytes 103809024 | tf_op jit(solution)/shard_map/dot_general | solution.py:66
  350.6 0.2 all-reduce.5.cloned.1.call-start
  350.9 243.4 %reduce-scatter.2.cloned.1.call-done = bf16[768,1024]{1,0:T(8,128)(2,1)} async-done(((bf16[12288,1024]{1,0:T(8,128)(2,1)}), bf16[768,1024]{1,0:T(8,128)(2,1)}) %reduce-scatter.2.cloned.1.call-update) | async-done | bytes 1572880 | tf_op jit(solution)/shard_map/reduce_scatter | solution.py:65
  594.3 1.8 convert_element_type.26
  596.1 0.2 fusion.10
  596.3 0.6 fusion.9
  596.9 3.0 fusion.14
  599.9 2.7 fusion.18
  602.6 2.7 fusion.16
  605.4 0.0 all-reduce.5.cloned.1.call-update
  605.4 2.6 copy.14
  608.0 135.7 %all-reduce.5.cloned.1.call-done = (f32[512,512]{1,0:T(8,128)}, f32[512,512]{1,0:T(8,128)}, f32[512,512]{0,1:T(8,128)}) async-done(((f32[512,512]{1,0:T(8,128)}, f32[512,512]{1,0:T(8,128)}, f32[512,512]{0,1:T(8,128)}), (f32[512,512]{1,0:T(8,128)}, f32[512,512]{1,0:T(8,128)}, f32[512,512]{0,1:T(8,128)})) %all-reduce.5.cloned.1.call-update) | async-done | bytes 3145744 | tf_op jit(solution)/shard_map/psum | solution.py:76
  743.7 1.6 sub.18
  745.3 1.0 fusion.11
  746.4 2.0 fusion.13
  748.4 2.5 copy.16
  (23 shorter events, 0.1 us)
Async XLA Ops:
  7.2 589.2 %copy-start = (bf16[512,512]{1,0:T(8,128)(2,1)S(1)}, bf16[512,512]{1,0:T(8,128)(2,1)}, u32[]{:S(2)}) copy-start(bf16[512,512]{1,0:T(8,128)(2,1)} %param.15) | copy-start | bytes 1572868
  7.2 106.8 %all-gather.5.cloned.1.call-start = ((), (), s32[]{:S(2)}) async-start(), calls=%async_computation.2 | async-start | bytes 13369344 | tf_op jit(solution)/shard_map/all_gather | solution.py:58
  10.2 205.4 %all-gather.3.cloned.1.call-start = ((), (), s32[]{:S(2)}) async-start(), calls=%async_computation.1 | async-start | bytes 13369344 | tf_op jit(solution)/shard_map/all_gather | solution.py:57
  12.4 290.3 %all-reduce.7.cloned.1.call-start = ((), (), s32[]{:S(2)}) async-start(), calls=%async_computation.5 | async-start | bytes 6291456 | tf_op jit(solution)/shard_map/psum | solution.py:11
  116.9 101.6 %copy-start.9 = (s32[64,64]{1,0:T(8,128)S(1)}, s32[64,64]{1,0:T(8,128)}, u32[]{:S(2)}) copy-start(s32[64,64]{1,0:T(8,128)} %param.10) | copy-start | bytes 49156
  218.4 375.9 %reduce-scatter.2.cloned.1.call-start = ((), (), s32[]{:S(2)}) async-start(), calls=%async_computation.3 | async-start | bytes 26738688 | tf_op jit(solution)/shard_map/reduce_scatter | solution.py:65
  350.6 393.1 %all-reduce.5.cloned.1.call-start = ((), (), s32[]{:S(2)}) async-start(), calls=%async_computation.4 | async-start | bytes 6291456 | tf_op jit(solution)/shard_map/psum | solution.py:76
  596.3 3.6 copy-start.1
  596.9 8.4 %copy-start.5 = (bf16[768,512]{1,0:T(8,128)(2,1)}, bf16[768,512]{1,0:T(8,128)(2,1)S(1)}, u32[]{:S(2)}) copy-start(bf16[768,512]{1,0:T(8,128)(2,1)S(1)} %fusion.9) | copy-start | bytes 2359300
  605.3 138.4 %copy-start.6 = (f32[512,512]{1,0:T(8,128)S(1)}, f32[512,512]{1,0:T(8,128)}, u32[]{:S(2)}) copy-start(f32[512,512]{1,0:T(8,128)} %param.16) | copy-start | bytes 3145732
  743.7 1.6 copy-start.7
  743.7 2.6 copy-start.4
  743.7 2.6 copy-start.8
  745.3 3.1 copy-start.2
  746.3 4.6 copy-start.3
Sparse Core Ops, SparseCore 0:
  10.8 103.1 all-gather.4
  116.9 98.6 all-gather.2
  218.5 84.0 all-reduce.6
  350.8 243.4 reduce-scatter.1
  605.5 138.1 all-reduce.4
where the time goes:
time: 758 us; the launch traced here: 757 us
  waiting for transfers between devices  623 us (82%)
  matrix products  59.9 us (8%)
  local copies, waits for them, and re-layouts  45.4 us (6%)
  other arithmetic  14.4 us (2%)
  between operations  14 us (2%)
    reduce_scatter x1, waiting for transfers between devices, body(): lax.psum_scatter(jnp.dot(sparse, stacked, preferred_element_type=jnp.floa...  243 us
    psum x1, waiting for transfers between devices, body(): lax.psum((jnp.dot(own_first.T, column_first, preferred_element_type=jnp.f...  136 us
    all_gather x1, waiting for transfers between devices, body(): lax.all_gather(local_second, 'pcol', axis=1, tiled=True)  102 us
    all_gather x1, waiting for transfers between devices, body(): lax.all_gather(local_first, 'pcol', axis=1, tiled=True)  98.7 us
    dot_general x1, matrix products, body(): jnp.dot(sparse, stacked, preferred_element_type=jnp.float32)  48 us
    psum x1, waiting for transfers between devices, from_root(): return lax.psum(jnp.where(mine, shard, jnp.zeros_like(shard)), axis)  43.9 us
    unnamed x23, local copies, waits for them, and re-layouts  31.3 us
  transfers between devices with their start and end apart: 5, of which 5 were waited for; matrix products, arithmetic and copies ran while one was open for 6% of the time, Pallas kernels for 0%

commit v1 on v0

v1 whole, which is shorter than its diff:
```python
import functools

import jax
import jax.numpy as jnp
from jax import lax
from jax.experimental import pallas as pl
from jax.experimental.pallas import tpu as pltpu
from jax.sharding import PartitionSpec as P


TILE = 384
BF = jnp.bfloat16
F32 = jnp.float32
BOTH = ("prow", "pcol")


PARAMS = pltpu.CompilerParams(vmem_limit_bytes=67043328)


def whole(*shape):
    return pl.BlockSpec(shape, lambda *_: (0,) * len(shape))


def product_kernel(start, half, count, meta_ref, pattern_ref, *refs):
    inverse_refs, panel_refs, outs = refs[:4], refs[4 : 4 + count], refs[-2 * count :]
    step = start + pl.program_id(0)
    tiles = inverse_refs[0].shape[1] // TILE
    for which, inverse_ref in enumerate(inverse_refs):
        tile_row = meta_ref[step * 4 + which] * half // TILE
        pieces = []
        for tile in range(tiles):
            keep = pattern_ref[tile_row * tiles + tile] != 0
            block = inverse_ref[:, tile * TILE : (tile + 1) * TILE]
            pieces.append(jnp.where(keep, block, jnp.zeros_like(block)))
        kept = jnp.concatenate(pieces, axis=1)
        for number, panel_ref in enumerate(panel_refs):
            product = lax.dot_general(
                kept, panel_ref[...], (((1,), (1,)), ((), ())), preferred_element_type=F32
            )
            outs[number + which // 2 * count][0, which % 2] = product.astype(BF)


def products(start, stop, meta, pattern, inverse, panels, half, after=()):
    width, depth = panels[0].shape
    wide = width * len(panels)
    count = stop - start
    spec = lambda which: pl.BlockSpec(
        (half, depth), lambda i, m, p: (m[(start + i) * 4 + which], 0)
    )
    out = jax.ShapeDtypeStruct((count, 2, half, width), BF)
    out_spec = pl.BlockSpec((1, 2, half, width), lambda i, m, p: (i, 0, 0, 0))
    return pl.pallas_call(
        functools.partial(product_kernel, start, half, len(panels)),
        out_shape=[out] * (2 * len(panels)),
        grid_spec=pltpu.PrefetchScalarGridSpec(
            num_scalar_prefetch=2,
            grid=(count,),
            in_specs=[spec(which) for which in range(4)]
            + [whole(width, depth)] * len(panels)
            + [pl.BlockSpec(memory_space=pl.ANY)] * len(after),
            out_specs=[out_spec] * (2 * len(panels)),
        ),
        cost_estimate=pl.CostEstimate(
            flops=8 * count * half * wide * depth,
            bytes_accessed=2 * (4 * count * half * (depth + wide) + wide * depth),
            transcendentals=0,
        ),
        compiler_params=PARAMS,
        name="products",
    )(meta, pattern, inverse, inverse, inverse, inverse, *panels, *after)


def add_kernel(arrived, last, *refs):
    own_ref, core_ref, outs = refs[0], refs[1], refs[2 + 2 * arrived :]
    for side in range(2):
        total = own_ref[0, side].astype(F32) + core_ref[0, side].astype(F32)
        if arrived:
            total = total + refs[2 + side][...].astype(F32)
        if last:
            outs[0][side] = total
        else:
            outs[side][...] = total.astype(BF)


def add(index, own, core_in, arrived, last):
    _, _, half, width = own.shape
    parts = 2 if half % 32 == 0 else 1
    rows = half // parts
    made = pl.BlockSpec((1, 2, rows, width), lambda i: (index, 0, i, 0))
    moving = pl.BlockSpec((rows, width), lambda i: (i, 0))
    if last:
        out_shape = [jax.ShapeDtypeStruct((2, half, width), F32)]
        out_specs = [pl.BlockSpec((2, rows, width), lambda i: (0, i, 0))]
    else:
        out_shape = [jax.ShapeDtypeStruct((half, width), BF)] * 2
        out_specs = [moving] * 2
    return pl.pallas_call(
        functools.partial(add_kernel, len(arrived) > 0, last),
        out_shape=out_shape,
        grid=(parts,),
        in_specs=[made, made] + [moving] * len(arrived),
        out_specs=out_specs,
        cost_estimate=pl.CostEstimate(
            flops=6 * half * width, bytes_accessed=16 * half * width, transcendentals=0
        ),
        compiler_params=PARAMS,
        name="add",
    )(own, core_in, *arrived)


def stages_of(rows, cols):
    def core(r, c):
        return c % 2, lambda m: (r, c - c % 2 + m)

    def near(r, c):
        return r * 2 + c // 2 % 2, lambda m: (m // 2, c - c % 4 + m % 2 * 2 + c % 2)

    def far(r, c):
        return c // 4, lambda m: (r, m * 4 + c % 4)

    return ((2, core), (rows * 2, near), (cols // 4, far))


def to_follower(value, rows, cols, members, group, shift):
    pairs = []
    for r in range(rows):
        for c in range(cols):
            at, member = group(r, c)
            to_r, to_c = member((at + shift) % members)
            pairs.append((r * cols + c, to_r * cols + to_c))
    return lax.ppermute(value, BOTH, pairs)


def cut_into(outs, total_ref, at):
    size = outs[0].shape[0]
    for place, out in enumerate(outs):
        start = lax.rem(at + place, len(outs)) * size
        if size % 8 == 0:
            start = pl.multiple_of(start, size)
        out[...] = total_ref[pl.ds(start, size), :].astype(BF)


def cut_kernel(members, at_ref, *refs):
    sources, outs = refs[: -members - 1], refs[-members - 1 : -1]
    total = sources[0][...].astype(F32)
    for source in sources[1:]:
        total = total + source[...].astype(F32)
    if members == 1:
        outs[0][...] = total.astype(BF)
    else:
        refs[-1][...] = total
        cut_into(outs, refs[-1], at_ref[0])


def cut(at, members, sources):
    rows, width = sources[0].shape
    size = rows // members
    return pl.pallas_call(
        functools.partial(cut_kernel, members),
        out_shape=[jax.ShapeDtypeStruct((size, width), BF)] * members,
        grid_spec=pltpu.PrefetchScalarGridSpec(
            num_scalar_prefetch=1,
            grid=(1,),
            in_specs=[whole(rows, width)] * len(sources),
            out_specs=[whole(size, width)] * members,
            scratch_shapes=[pltpu.VMEM((rows, width), F32)],
        ),
        compiler_params=PARAMS,
        name="cut",
    )(at[None], *sources)


def place_into(out_ref, pieces, at):
    size = pieces[0].shape[0]
    for place, ref in enumerate(pieces):
        start = lax.rem(at + place, len(pieces)) * size
        if size % 16 == 0:
            start = pl.multiple_of(start, size)
        out_ref[pl.ds(start, size), :] = ref[...].astype(out_ref.dtype)


def place_kernel(at_ref, *refs):
    place_into(refs[-1], refs[:-1], at_ref[0])


def place_all(at, pieces):
    size, width = pieces[0].shape
    shape = (len(pieces) * size, width)
    return pl.pallas_call(
        place_kernel,
        out_shape=jax.ShapeDtypeStruct(shape, BF if size % 16 == 0 else F32),
        grid_spec=pltpu.PrefetchScalarGridSpec(
            num_scalar_prefetch=1,
            grid=(1,),
            in_specs=[whole(size, width)] * len(pieces),
            out_specs=whole(*shape),
        ),
        compiler_params=PARAMS,
        name="place",
    )(at[None], *pieces).astype(BF)


def first_kernel(at_ref, ends_ref, p1_ref, p2_ref, inner_ref, column_ref, lead_ref, *refs):
    width = inner_ref.shape[0]
    column = (-ends_ref[...]).astype(BF)
    column_ref[...] = column
    lead_ref[...] = jnp.dot(column, inner_ref[...], preferred_element_type=F32)
    refs[-1][:width] = jnp.dot(p1_ref[...], column, preferred_element_type=F32)
    refs[-1][width:] = jnp.dot(p2_ref[...], column, preferred_element_type=F32)
    cut_into(refs[:-1], refs[-1], at_ref[0])


def first_column(at, ends, p1, p2, inner):
    share, width = ends.shape
    return pl.pallas_call(
        first_kernel,
        out_shape=[
            jax.ShapeDtypeStruct((share, width), BF),
            jax.ShapeDtypeStruct((share, width), F32),
            jax.ShapeDtypeStruct((width, width), BF),
            jax.ShapeDtypeStruct((width, width), BF),
        ],
        grid_spec=pltpu.PrefetchScalarGridSpec(
            num_scalar_prefetch=1,
            grid=(1,),
            in_specs=[whole(share, width), whole(width, share), whole(width, share), whole(width, width)],
            out_specs=[whole(share, width)] * 2 + [whole(width, width)] * 2,
            scratch_shapes=[pltpu.VMEM((2 * width, width), F32)],
        ),
        compiler_params=PARAMS,
        name="first_column",
    )(at[None], ends, p1, p2, inner)


def second_kernel(at_ref, ends_ref, lead_ref, p2_ref, column_ref, *refs):
    column = (-(ends_ref[...] + lead_ref[...])).astype(BF)
    column_ref[...] = column
    refs[-1][...] = jnp.dot(p2_ref[...], column, preferred_element_type=F32)
    cut_into(refs[:-1], refs[-1], at_ref[0])


def second_column(at, ends, lead, p2):
    share, width = ends.shape
    return pl.pallas_call(
        second_kernel,
        out_shape=[
            jax.ShapeDtypeStruct((share, width), BF),
            jax.ShapeDtypeStruct((width // 2, width), BF),
            jax.ShapeDtypeStruct((width // 2, width), BF),
        ],
        grid_spec=pltpu.PrefetchScalarGridSpec(
            num_scalar_prefetch=1,
            grid=(1,),
            in_specs=[whole(share, width), whole(share, width), whole(width, share)],
            out_specs=[whole(share, width)] + [whole(width // 2, width)] * 2,
            scratch_shapes=[pltpu.VMEM((width, width), F32)],
        ),
        compiler_params=PARAMS,
        name="second_column",
    )(at[None], ends, lead, p2)


def sharp(left, right):
    high = left.astype(BF)
    rest = left - high.astype(F32)
    middle = rest.astype(BF)
    low = (rest - middle.astype(F32)).astype(BF)
    dot = lambda part: jnp.dot(part, right, preferred_element_type=F32)
    return dot(low) + dot(middle) + dot(high)


def close_kernel(at_ref, low_ref, high_ref, first_ref, second_ref, inner_ref, *refs):
    diagonal_ref, cross_ref, base_ref, sums_ref = refs
    place_into(sums_ref, (low_ref, high_ref), at_ref[0])
    width = inner_ref.shape[0]
    diagonal = first_ref[...] - sums_ref[:width]
    diagonal_ref[...] = diagonal
    cross = -(sharp(diagonal, inner_ref[...]) + sums_ref[width:].T)
    cross_ref[...] = cross
    base_ref[...] = second_ref[...] - sharp(cross.T, inner_ref[...]).T


def close(at, pieces, pivot_first, pivot_second, inner_panel):
    width = inner_panel.shape[0]
    square = whole(width, width)
    return pl.pallas_call(
        close_kernel,
        out_shape=[jax.ShapeDtypeStruct((width, width), F32)] * 3,
        grid_spec=pltpu.PrefetchScalarGridSpec(
            num_scalar_prefetch=1,
            grid=(1,),
            in_specs=[square] * 5,
            out_specs=[square] * 3,
            scratch_shapes=[pltpu.VMEM((2 * width, width), F32)],
        ),
        compiler_params=PARAMS,
        name="close",
    )(at[None], *pieces, pivot_first, pivot_second, inner_panel)


def last_kernel(at_ref, low_ref, high_ref, base_ref, out_ref):
    place_into(out_ref, (low_ref, high_ref), at_ref[0])
    out_ref[...] = base_ref[...] - out_ref[...]


def last(at, pieces, base):
    width = base.shape[0]
    part = whole(width // 2, width)
    return pl.pallas_call(
        last_kernel,
        out_shape=jax.ShapeDtypeStruct((width, width), F32),
        grid_spec=pltpu.PrefetchScalarGridSpec(
            num_scalar_prefetch=1,
            grid=(1,),
            in_specs=[part, part, whole(width, width)],
            out_specs=whole(width, width),
        ),
        compiler_params=PARAMS,
        name="last",
    )(at[None], *pieces, base)


def plan(chips):
    make = lambda rings, start, stop: ("make", rings, start, min(stop, chips))
    step = lambda kind, ring, at: (kind, (ring,), at, at + 1)
    events = [make((0,), 0, 1), step("add", 0, 0), make((0,), 1, 3), step("add", 0, 1)]
    events += [make((0,), 3, 4), step("add", 0, 2), make((1,), 0, 4), step("add", 1, 0)]
    made = 4
    for at in range(3, chips):
        events.append(step("add", 0, at))
        if made < chips:
            events.append(make((0, 1), made, made + 2))
            made += 2
        events.append(step("add", 1, at - 2))
    events += [step("sum", 0, 0), step("add", 1, chips - 2), step("sum", 0, 1)]
    events += [step("add", 1, chips - 1), step("sum", 1, 0), step("sum", 0, 2)]
    for at in range(1, 6):
        events.append(step("sum", 1, at))
        if at < 4:
            events.append(step("sum", 0, at + 2))
    return events


def body(
    ancestor_inverse,
    tile_pattern,
    rows_first,
    rows_second,
    panel_first,
    panel_second,
    inner_panel,
    pivot_first,
    pivot_second,
):
    rows, cols = lax.axis_size("prow"), lax.axis_size("pcol")
    row_id, col_id = lax.axis_index("prow"), lax.axis_index("pcol")
    row_block, col_block = ancestor_inverse.shape
    share = row_block // cols
    half = share // 2
    width = inner_panel.shape[0]
    local = panel_first.shape[1]
    piece = local // rows
    chips = cols // 2

    tile_rows, tile_cols = row_block // TILE, col_block // TILE
    pattern = lax.dynamic_slice(
        tile_pattern, (row_id * tile_rows, col_id * tile_cols), (tile_rows, tile_cols)
    ).reshape(-1)
    chip, core = col_id // 2, col_id % 2
    place = jnp.where(chip % 2 == 0, chip // 2, chips - 1 - chip // 2)
    steps = jnp.arange(chips, dtype=jnp.int32)
    dest = jnp.stack([(place - 1 - steps) % chips, (place + 1 + steps) % chips], axis=1)
    dest = jnp.where(dest < chips // 2, 2 * dest, 2 * (chips - 1 - dest) + 1)
    side = jnp.arange(2, dtype=jnp.int32)[None, :]
    meta = jnp.concatenate(
        [(dest * 2 + core) * 2 + side, (dest * 2 + 1 - core) * 2 + side], axis=1
    ).reshape(-1)
    order = [2 * i if i < chips // 2 else 2 * (chips - 1 - i) + 1 for i in range(chips)]
    onward = [
        (order[i] * 2 + k, order[(i + 1) % chips] * 2 + k) for i in range(chips) for k in range(2)
    ]
    backward = [(b, a) for a, b in onward]
    swap = [(c, c ^ 1) for c in range(cols)]
    to_share = [
        (a * cols + k, k * rows + (a + 1) % rows) for a in range(rows) for k in range(cols)
    ]

    struct_first = lax.dynamic_slice_in_dim(rows_first, row_id * row_block, row_block).astype(BF)
    struct_second = struct_first * lax.dynamic_slice_in_dim(
        rows_second, row_id * row_block, row_block
    ).astype(BF)

    def spread(panel, struct):
        turned = (panel.T * struct[None, :]).reshape(rows, piece, row_block)
        gathered = jnp.zeros((rows, cols // rows, piece, col_block), BF)
        for shift in range(rows):
            part = lax.dynamic_index_in_dim(turned, (row_id + shift) % rows, 0, keepdims=False)
            if shift:
                part = lax.ppermute(part, "prow", [(a, (a + shift) % rows) for a in range(rows)])
            part = part.reshape(piece, cols // rows, col_block).transpose(1, 0, 2)
            gathered = lax.dynamic_update_index_in_dim(gathered, part, (row_id - shift) % rows, 0)
        return gathered.reshape(cols, piece, col_block)

    def exchange(gathered):
        return lax.all_to_all(gathered, "pcol", 0, 0, tiled=True)

    def complete(mine):
        full = jnp.zeros((cols, rows, piece, col_block), BF)
        for shift in range(rows):
            part = mine
            if shift:
                part = lax.ppermute(part, "prow", [(a, (a - shift) % rows) for a in range(rows)])
            full = lax.dynamic_update_index_in_dim(full, part, (row_id + shift) % rows, 1)
        return full.reshape(width, col_block)

    gathered = [spread(panel_first, struct_first), spread(panel_second, struct_second)]
    mine_first = exchange(gathered[0])
    mine_second = exchange(gathered[1])
    panels = [complete(mine_first)]
    panels.append(complete(mine_second))

    own_rows = []
    for number, panel in enumerate(panels):
        own_rows.append(
            lax.ppermute(
                lax.dynamic_slice_in_dim(panel, (row_id + 1) % rows * share, share, 1),
                BOTH,
                to_share,
            )
        )

    made, arrived, ends, summed = [[], []], [[], []], [None, None], [None, None]
    places = (col_id % 2, row_id * 2 + (col_id // 2) % 2, col_id // 4)
    stages = list(zip(stages_of(rows, cols), places))
    for event in plan(chips):
        kind, rings, start, stop = event
        if kind == "make":
            made_now = products(
                start,
                stop,
                meta,
                pattern,
                ancestor_inverse,
                [panels[r] for r in rings],
                half,
                (mine_second,) if rings == (0,) and start == 1 else (),
            )
            theirs = [lax.ppermute(p, "pcol", swap) for p in made_now[len(rings) :]]
            for column, ring in enumerate(rings):
                made[ring] += [(i, made_now[column], theirs[column]) for i in range(stop - start)]
        elif kind == "add":
            ring = rings[0]
            total = add(*made[ring][start], arrived[ring], start == chips - 1)
            if start == chips - 1:
                ends[ring] = total[0].reshape(share, width)
            else:
                arrived[ring] = [
                    lax.ppermute(total[0], "pcol", onward),
                    lax.ppermute(total[1], "pcol", backward),
                ]
        else:
            ring, number = rings[0], start
            (members, group), at = stages[min(number, 5 - number)]
            if number == 0 and ring == 0:
                column_first, lead, *cuts = first_column(at, ends[0], *own_rows, inner_panel)
            elif number == 0:
                column_second, *cuts = second_column(at, ends[1], lead, own_rows[1])
            elif number == 1:
                cuts = cut(at, members, summed[ring])
            elif number < 4:
                cuts = cut(at, 1, summed[ring])
            elif number == 4:
                cuts = [place_all(stages[1][1], summed[ring])]
            elif ring == 0:
                diagonal_first, inner_second, base = close(
                    at, summed[0], pivot_first, pivot_second, inner_panel
                )
            else:
                diagonal_second = last(at, summed[1], base)
            if number < 5:
                (members, group), _ = stages[(0, 1, 2, 1, 0)[number]]
                summed[ring] = [cuts[0]] + [
                    to_follower(
                        cuts[shift] if number < 2 else cuts[0],
                        rows,
                        cols,
                        members,
                        group,
                        shift if number < 2 else members - shift,
                    )
                    for shift in range(1, members)
                ]
    return (column_first, diagonal_first, inner_second, column_second, diagonal_second)


def solution(mesh):
    return jax.shard_map(
        body,
        mesh=mesh,
        in_specs=(
            P("prow", "pcol"),
            P(),
            P(),
            P(),
            P("prow", "pcol"),
            P("prow", "pcol"),
            P(),
            P(),
            P(),
        ),
        out_specs=(P(("prow", "pcol"), None), P(), P(), P(("prow", "pcol"), None), P()),
        check_vma=False,
    )
```

time: 758 us -> 386 us (0.51)
  waiting for transfers between devices: 623 us -> 113 us
  Pallas kernels: 0 us -> 141 us
  starting transfers between devices: 0.39 us -> 106 us
  matrix products: 59.9 us -> 0 us
  local copies, waits for them, and re-layouts: 45.4 us -> 20.4 us
  between operations: 14 us -> 0.9 us
  other arithmetic: 14.4 us -> 2.47 us
    reduce_scatter x1 -> x0, waiting for transfers between devices: 243 us -> none  [body(): lax.psum_scatter(jnp.dot(sparse, stacked, preferred_element_type=jnp.floa...]
    all_gather x2 -> x0, waiting for transfers between devices: 200 us -> none  [the longest x1 102 us: body(): lax.all_gather(local_second, 'pcol', axis=1, tiled=True)]
    psum x2 -> x0, waiting for transfers between devices: 180 us -> none  [the longest x1 136 us: body(): lax.psum((jnp.dot(own_first.T, column_first, preferred_element_type=jnp.f...]
    pallas_call x0 -> x34, Pallas kernels: none -> 141 us  [the longest x6 71.8 us: products(): pl.pallas_call(functools.partial(product_kernel, start, half, len(panels)...]
    ppermute x0 -> x64, starting transfers between devices: none -> 94.8 us  [the longest x14 47.5 us: body(): lax.ppermute(total[0], 'pcol', onward)]
    ppermute x0 -> x64, waiting for transfers between devices: none -> 91.5 us  [the longest x22 29.6 us: to_follower(): return lax.ppermute(value, BOTH, pairs)]
    dot_general x7 -> x0, matrix products: 59.9 us -> none  [the longest x1 48 us: body(): jnp.dot(sparse, stacked, preferred_element_type=jnp.float32)]
    unnamed x23 -> x8, local copies, waits for them, and re-layouts: 31.3 us -> 0.48 us
  transfers between devices with their start and end apart: 5 -> 66, of which waited for: 5 -> 32; matrix products, arithmetic and copies ran while one was open for 6% -> 5% of each run, Pallas kernels for 0% -> 36%
where the time goes in v1:
time: 386 us; the launch traced here: 384 us
  Pallas kernels  141 us (37%)
  waiting for transfers between devices  113 us (29%)
  starting transfers between devices  106 us (27%)
  local copies, waits for them, and re-layouts  20.4 us (5%)
    pallas_call x6, Pallas kernels, products(): pl.pallas_call(functools.partial(product_kernel, start, half, len(panels)...  71.8 us
    ppermute x14, starting transfers between devices, body(): lax.ppermute(total[0], 'pcol', onward)  47.5 us
    pallas_call x16, Pallas kernels, add(): pl.pallas_call(functools.partial(add_kernel, len(arrived) > 0, last), out...  38.6 us
    ppermute x22, waiting for transfers between devices, to_follower(): return lax.ppermute(value, BOTH, pairs)  29.6 us
    ppermute x14, waiting for transfers between devices, body(): lax.ppermute(total[1], 'pcol', backward)  23.3 us
    ppermute x22, starting transfers between devices, to_follower(): return lax.ppermute(value, BOTH, pairs)  22.6 us
    all_to_all x2, waiting for transfers between devices, exchange(): return lax.all_to_all(gathered, 'pcol', 0, 0, tiled=True)  21.7 us
    ppermute x14, waiting for transfers between devices, body(): lax.ppermute(total[0], 'pcol', onward)  20.9 us
  transfers between devices with their start and end apart: 66, of which 32 were waited for; matrix products, arithmetic and copies ran while one was open for 5% of the time, Pallas kernels for 36%

profile of v1, /device:TPU:0, one launch (start us, length us, event | category | flops | bytes accessed | tf_op | source)
XLA Modules:
  0.0 384.3 jit_solution(7979607991871591667)
XLA Ops:
  3.2 3.1 collective-permute-start.2
  8.2 7.2 %collective-permute-done.2 = bf16[16,12288]{1,0:T(8,128)(2,1)S(1)} collective-permute-done((bf16[16,12288]{1,0:T(8,128)(2,1)S(1)}, bf16[16,12288]{1,0:T(8,128)(2,1)S(1)}, u32[]{:S(2)}, u32[]{:S(2)}) %collective-permute-start.2) | collective-permute-done | bytes 393248 | tf_op jit(solution)/shard_map/ppermute | solution.py:399
  16.3 6.1 %all-to-all-start.1 = ((bf16[16,16,1536]{2,1,0:T(8,128)(2,1)}), bf16[16,16,1536]{2,1,0:T(8,128)(2,1)S(1)}, u32[]{:S(2)}, u32[]{:S(2)}) async-start(bf16[16,16,1536]{2,1,0:T(8,128)(2,1)} %bitcast.22), calls=%async_computation.1 | async-start | bytes 1572864 | tf_op jit(solution)/shard_map/all_to_all | solution.py:405
  26.1 8.0 %collective-permute-done = bf16[16,12288]{1,0:T(8,128)(2,1)S(1)} collective-permute-done((bf16[16,12288]{1,0:T(8,128)(2,1)S(1)}, bf16[16,12288]{1,0:T(8,128)(2,1)S(1)}, u32[]{:S(2)}, u32[]{:S(2)}) %collective-permute-start) | collective-permute-done | bytes 393248 | tf_op jit(solution)/shard_map/ppermute | solution.py:399
  35.0 6.1 %all-to-all-done.1.refs_5_ = bf16[16,16,1536]{2,1,0:T(8,128)(2,1)S(1)} async-done(((bf16[16,16,1536]{2,1,0:T(8,128)(2,1)}), bf16[16,16,1536]{2,1,0:T(8,128)(2,1)S(1)}, u32[]{:S(2)}, u32[]{:S(2)}) %all-to-all-start.1) | async-done | bytes 786464 | tf_op jit(solution)/shard_map/all_to_all | solution.py:405
  41.1 5.4 %all-to-all-start = ((bf16[16,16,1536]{2,1,0:T(8,128)(2,1)}), bf16[16,16,1536]{2,1,0:T(8,128)(2,1)}, u32[]{:S(2)}, u32[]{:S(2)}) async-start(bf16[16,16,1536]{2,1,0:T(8,128)(2,1)} %bitcast.9), calls=%async_computation | async-start | bytes 1572864 | tf_op jit(solution)/shard_map/all_to_all | solution.py:405
  49.7 15.6 %all-to-all-done = bf16[16,16,1536]{2,1,0:T(8,128)(2,1)} async-done(((bf16[16,16,1536]{2,1,0:T(8,128)(2,1)}), bf16[16,16,1536]{2,1,0:T(8,128)(2,1)}, u32[]{:S(2)}, u32[]{:S(2)}) %all-to-all-start) | async-done | bytes 786464 | tf_op jit(solution)/shard_map/all_to_all | solution.py:405
  70.0 15.5 %products.11 = (bf16[4,2,384,512]{3,2,1,0:T(8,128)(2,1)}, bf16[4,2,384,512]{3,2,1,0:T(8,128)(2,1)}) custom-call(s32[32]{0:T(128)} %reshape.136.meta_ref, s32[128]{0:T(128)} %reshape.137.pattern_ref, bf16[12288,1536]{1,0:T(8,128)(2,1)} %refs_3_.11, bf16[12288,1536]{1,0:T(8,128)(2,1)} %refs_3_.11, bf16[12288,1536]{1,0:T(8,128)(2,1)} %refs_3_.11, ...), custom_call_target="tpu_custom_call" | custom-call | flops 9663676416 | bytes 26738688 | tf_op jit(solution)/shard_map/products/pallas_call | solution.py:52
  91.3 10.1 %products.9 = (bf16[2,2,384,512]{3,2,1,0:T(8,128)(2,1)}, bf16[2,2,384,512]{3,2,1,0:T(8,128)(2,1)}) custom-call(s32[32]{0:T(128)} %reshape.136.meta_ref, s32[128]{0:T(128)} %reshape.137.pattern_ref, bf16[12288,1536]{1,0:T(8,128)(2,1)} %refs_3_.11, bf16[12288,1536]{1,0:T(8,128)(2,1)} %refs_3_.11, bf16[12288,1536]{1,0:T(8,128)(2,1)} %refs_3_.11, ...), custom_call_target="tpu_custom_call" | custom-call | flops 4831838208 | bytes 14155776 | tf_op jit(solution)/shard_map/products/pallas_call | solution.py:52
  101.9 7.0 %products.10 = (bf16[1,2,384,512]{3,2,1,0:T(8,128)(2,1)}, bf16[1,2,384,512]{3,2,1,0:T(8,128)(2,1)}) custom-call(s32[32]{0:T(128)} %reshape.136.meta_ref, s32[128]{0:T(128)} %reshape.137.pattern_ref, bf16[12288,1536]{1,0:T(8,128)(2,1)} %refs_3_.11, bf16[12288,1536]{1,0:T(8,128)(2,1)} %refs_3_.11, bf16[12288,1536]{1,0:T(8,128)(2,1)} %refs_3_.11, ...), custom_call_target="tpu_custom_call" | custom-call | flops 2415919104 | bytes 7864320 | tf_op jit(solution)/shard_map/products/pallas_call | solution.py:52
  108.9 2.6 collective-permute-done.8.refs_1_
  116.0 9.9 %collective-permute-done.10.refs_3_ = bf16[384,512]{1,0:T(8,128)(2,1)} collective-permute-done((bf16[384,512]{1,0:T(8,128)(2,1)}, bf16[384,512]{1,0:T(8,128)(2,1)}, u32[]{:S(2)}, u32[]{:S(2)}) %collective-permute-start.10) | collective-permute-done | bytes 393248 | tf_op jit(solution)/shard_map/ppermute | solution.py:459
  131.4 7.0 %products.8 = (bf16[1,2,384,512]{3,2,1,0:T(8,128)(2,1)}, bf16[1,2,384,512]{3,2,1,0:T(8,128)(2,1)}) custom-call(s32[32]{0:T(128)} %reshape.136.meta_ref, s32[128]{0:T(128)} %reshape.137.pattern_ref, bf16[12288,1536]{1,0:T(8,128)(2,1)} %refs_3_.11, bf16[12288,1536]{1,0:T(8,128)(2,1)} %refs_3_.11, bf16[12288,1536]{1,0:T(8,128)(2,1)} %refs_3_.11, ...), custom_call_target="tpu_custom_call" | custom-call | flops 2415919104 | bytes 7864320 | tf_op jit(solution)/shard_map/products/pallas_call | solution.py:52
  148.8 16.0 %products.7 = (bf16[2,2,384,512]{3,2,1,0:T(8,128)(2,1)}, bf16[2,2,384,512]{3,2,1,0:T(8,128)(2,1)}, bf16[2,2,384,512]{3,2,1,0:T(8,128)(2,1)}, bf16[2,2,384,512]{3,2,1,0:T(8,128)(2,1)}) custom-call(s32[32]{0:T(128)} %reshape.136.meta_ref, s32[128]{0:T(128)} %reshape.137.pattern_ref, bf16[12288,1536]{1,0:T(8,128)(2,1)} %refs_3_.11, ...), custom_call_target="tpu_custom_call" | custom-call | flops 9663676416 | bytes 18874368 | tf_op jit(solution)/shard_map/products/pallas_call | solution.py:52
  170.4 16.0 %products.6 = (bf16[2,2,384,512]{3,2,1,0:T(8,128)(2,1)}, bf16[2,2,384,512]{3,2,1,0:T(8,128)(2,1)}, bf16[2,2,384,512]{3,2,1,0:T(8,128)(2,1)}, bf16[2,2,384,512]{3,2,1,0:T(8,128)(2,1)}) custom-call(s32[32]{0:T(128)} %reshape.136.meta_ref, s32[128]{0:T(128)} %reshape.137.pattern_ref, bf16[12288,1536]{1,0:T(8,128)(2,1)} %refs_3_.11, ...), custom_call_target="tpu_custom_call" | custom-call | flops 9663676416 | bytes 18874368 | tf_op jit(solution)/shard_map/products/pallas_call | solution.py:52
  194.9 6.4 %collective-permute-done.15.refs_2_ = bf16[384,512]{1,0:T(8,128)(2,1)} collective-permute-done((bf16[384,512]{1,0:T(8,128)(2,1)}, bf16[384,512]{1,0:T(8,128)(2,1)}, u32[]{:S(2)}, u32[]{:S(2)}) %collective-permute-start.15) | collective-permute-done | bytes 393248 | tf_op jit(solution)/shard_map/ppermute | solution.py:458
  205.8 3.9 %collective-permute-done.43.refs_2_ = bf16[384,512]{1,0:T(8,128)(2,1)} collective-permute-done((bf16[384,512]{1,0:T(8,128)(2,1)}, bf16[384,512]{1,0:T(8,128)(2,1)}, u32[]{:S(2)}, u32[]{:S(2)}) %collective-permute-start.43) | collective-permute-done | bytes 393248 | tf_op jit(solution)/shard_map/ppermute | solution.py:458
  246.7 2.9 collective-permute-start.22
  253.2 32.3 %collective-permute-start.49 = (bf16[384,512]{1,0:T(8,128)(2,1)}, bf16[384,512]{1,0:T(8,128)(2,1)}, u32[]{:S(2)}, u32[]{:S(2)}) collective-permute-start(bf16[384,512]{1,0:T(8,128)(2,1)} %get-tuple-element.116), channel_id=1, source_target_pairs={{0,4},{1,5},{4,8},{5,9},{8,12},{9,13},{12,14},{13,15},{14,10},{15,... | collective-permute-start | bytes 1179656 | tf_op jit(solution)/shard_map/ppermute | solution.py:458
  285.5 2.7 collective-permute-done.22.refs_3_
  288.1 2.6 add.225
  290.8 4.5 %first_column.1 = (bf16[768,512]{1,0:T(8,128)(2,1)}, f32[768,512]{1,0:T(8,128)}, bf16[512,512]{1,0:T(8,128)(2,1)}, bf16[512,512]{1,0:T(8,128)(2,1)}) custom-call(s32[1]{0:T(128)} %bitcast.at_ref, f32[768,512]{1,0:T(8,128)} %bitcast.59, bf16[512,768]{1,0:T(8,128)(2,1)} %collective-permute-done.23.p1_ref, bf16[512,768]{1,0:T(8,128)(2,1)} %collective-permute-done.24.p2_ref, ...), custom_call_target="tpu_custom_call" | custom-call | tf_op jit(solution)/shard_map/first_column/pallas_call | solution.py:215
  295.5 3.7 collective-permute-done.50.refs_3_
  309.4 6.8 %collective-permute-done.26.refs_1_ = bf16[128,512]{1,0:T(8,128)(2,1)} collective-permute-done((bf16[128,512]{1,0:T(8,128)(2,1)}, bf16[128,512]{1,0:T(8,128)(2,1)}, u32[]{:S(2)}, u32[]{:S(2)}) %collective-permute-start.26) | collective-permute-done | bytes 131104 | tf_op jit(solution)/shard_map/ppermute | solution.py:131
  319.2 3.2 collective-permute-start.29
  323.0 2.6 add.233
  325.6 3.6 second_column.1
  335.8 4.1 %collective-permute-done.32.refs_1_ = bf16[128,512]{1,0:T(8,128)(2,1)} collective-permute-done((bf16[128,512]{1,0:T(8,128)(2,1)}, bf16[128,512]{1,0:T(8,128)(2,1)}, u32[]{:S(2)}, u32[]{:S(2)}) %collective-permute-start.32) | collective-permute-done | bytes 131104 | tf_op jit(solution)/shard_map/ppermute | solution.py:131
  346.9 2.9 collective-permute-start.56
  359.2 4.7 %collective-permute-done.58.refs_2_ = bf16[64,512]{1,0:T(8,128)(2,1)} collective-permute-done((bf16[64,512]{1,0:T(8,128)(2,1)}, bf16[64,512]{1,0:T(8,128)(2,1)}, u32[]{:S(2)}, u32[]{:S(2)}) %collective-permute-start.58) | collective-permute-done | bytes 65568 | tf_op jit(solution)/shard_map/ppermute | solution.py:131
  376.2 5.5 %close.1 = (f32[512,512]{1,0:T(8,128)}, f32[512,512]{1,0:T(8,128)}, f32[512,512]{1,0:T(8,128)}) custom-call(s32[1]{0:T(128)} %bitcast.at_ref, bf16[512,512]{1,0:T(8,128)(2,1)} %place.2.low_ref, bf16[512,512]{1,0:T(8,128)(2,1)} %collective-permute-done.35.high_ref, f32[512,512]{1,0:T(8,128)} %first_ref.1, f32[512,512]{1,0:T(8,128)} %second_ref.1, ...), custom_call_target="tpu_custom_call" | custom-call | tf_op jit(solution)/shard_map/close/pallas_call | solution.py:286
  381.8 2.5 last.1
  (167 shorter events, 152.7 us)
Async XLA Ops:
  16.3 24.8 %all-to-all-start.1 = ((bf16[16,16,1536]{2,1,0:T(8,128)(2,1)}), bf16[16,16,1536]{2,1,0:T(8,128)(2,1)S(1)}, u32[]{:S(2)}, u32[]{:S(2)}) async-start(bf16[16,16,1536]{2,1,0:T(8,128)(2,1)} %bitcast.22), calls=%async_computation.1 | async-start | bytes 1572864 | tf_op jit(solution)/shard_map/all_to_all | solution.py:405
  41.1 24.2 %all-to-all-start = ((bf16[16,16,1536]{2,1,0:T(8,128)(2,1)}), bf16[16,16,1536]{2,1,0:T(8,128)(2,1)}, u32[]{:S(2)}, u32[]{:S(2)}) async-start(bf16[16,16,1536]{2,1,0:T(8,128)(2,1)} %bitcast.9), calls=%async_computation | async-start | bytes 1572864 | tf_op jit(solution)/shard_map/all_to_all | solution.py:405
  46.6 22.5 %collective-permute-start.3 = (bf16[16,16,1536]{2,1,0:T(8,128)(2,1)S(1)}, bf16[16,16,1536]{2,1,0:T(8,128)(2,1)S(1)}, u32[]{:S(2)}, u32[]{:S(2)}) collective-permute-start(bf16[16,16,1536]{2,1,0:T(8,128)(2,1)S(1)} %all-to-all-done.1.refs_5_), channel_id=1, source_target_pairs={{0,16},{16,0},{1,17},{17,1},{2,18},{18,2},{3,19},{19,3},{4,20},{20... | collective-permute-start | bytes 2359304 | tf_op jit(solution)/shard_map/ppermute | solution.py:412
  65.3 23.9 %collective-permute-start.1 = (bf16[16,16,1536]{2,1,0:T(8,128)(2,1)}, bf16[16,16,1536]{2,1,0:T(8,128)(2,1)}, u32[]{:S(2)}, u32[]{:S(2)}) collective-permute-start(bf16[16,16,1536]{2,1,0:T(8,128)(2,1)} %all-to-all-done), channel_id=1, source_target_pairs={{0,16},{16,0},{1,17},{17,1},{2,18},{18,2},{3,19},{19,3},{4,20},{20... | collective-permute-start | bytes 2359304 | tf_op jit(solution)/shard_map/ppermute | solution.py:412
  85.6 59.0 %collective-permute-start.38 = (bf16[4,2,384,512]{3,2,1,0:T(8,128)(2,1)}, bf16[4,2,384,512]{3,2,1,0:T(8,128)(2,1)}, u32[]{:S(2)}, u32[]{:S(2)}) collective-permute-start(bf16[4,2,384,512]{3,2,1,0:T(8,128)(2,1)} %get-tuple-element.105), channel_id=1, source_target_pairs={{0,1},{1,0},{2,3},{3,2},{4,5},{5,4},{6,7},{7,6},{8,9},{9,8},{10,11... | collective-permute-start | bytes 9437192 | tf_op jit(solution)/shard_map/ppermute | solution.py:448
  101.4 25.5 %collective-permute-start.7 = (bf16[2,2,384,512]{3,2,1,0:T(8,128)(2,1)}, bf16[2,2,384,512]{3,2,1,0:T(8,128)(2,1)}, u32[]{:S(2)}, u32[]{:S(2)}) collective-permute-start(bf16[2,2,384,512]{3,2,1,0:T(8,128)(2,1)} %get-tuple-element.74), channel_id=1, source_target_pairs={{0,1},{1,0},{2,3},{3,2},{4,5},{5,4},{6,7},{7,6},{8,9},{9,8},{10,11... | collective-permute-start | bytes 4718600 | tf_op jit(solution)/shard_map/ppermute | solution.py:448
  113.7 12.3 %collective-permute-start.10 = (bf16[384,512]{1,0:T(8,128)(2,1)}, bf16[384,512]{1,0:T(8,128)(2,1)}, u32[]{:S(2)}, u32[]{:S(2)}) collective-permute-start(bf16[384,512]{1,0:T(8,128)(2,1)} %get-tuple-element.78), channel_id=1, source_target_pairs={{4,0},{5,1},{8,4},{9,5},{12,8},{13,9},{14,12},{15,13},{10,14},{11,... | collective-permute-start | bytes 1179656 | tf_op jit(solution)/shard_map/ppermute | solution.py:459
  138.4 29.9 %collective-permute-start.6 = (bf16[1,2,384,512]{3,2,1,0:T(8,128)(2,1)}, bf16[1,2,384,512]{3,2,1,0:T(8,128)(2,1)}, u32[]{:S(2)}, u32[]{:S(2)}) collective-permute-start(bf16[1,2,384,512]{3,2,1,0:T(8,128)(2,1)} %get-tuple-element.72), channel_id=1, source_target_pairs={{0,1},{1,0},{2,3},{3,2},{4,5},{5,4},{6,7},{7,6},{8,9},{9,8},{10,11... | collective-permute-start | bytes 2359304 | tf_op jit(solution)/shard_map/ppermute | solution.py:448
  143.1 26.7 %collective-permute-start.13 = (bf16[384,512]{1,0:T(8,128)(2,1)}, bf16[384,512]{1,0:T(8,128)(2,1)}, u32[]{:S(2)}, u32[]{:S(2)}) collective-permute-start(bf16[384,512]{1,0:T(8,128)(2,1)} %get-tuple-element.81), channel_id=1, source_target_pairs={{0,4},{1,5},{4,8},{5,9},{8,12},{9,13},{12,14},{13,15},{14,10},{15,... | collective-permute-start | bytes 1179656 | tf_op jit(solution)/shard_map/ppermute | solution.py:458
  146.7 18.1 %collective-permute-start.39 = (bf16[384,512]{1,0:T(8,128)(2,1)}, bf16[384,512]{1,0:T(8,128)(2,1)}, u32[]{:S(2)}, u32[]{:S(2)}) collective-permute-start(bf16[384,512]{1,0:T(8,128)(2,1)} %get-tuple-element.106), channel_id=1, source_target_pairs={{0,4},{1,5},{4,8},{5,9},{8,12},{9,13},{12,14},{13,15},{14,10},{15,... | collective-permute-start | bytes 1179656 | tf_op jit(solution)/shard_map/ppermute | solution.py:458
  148.2 17.1 %collective-permute-start.40 = (bf16[384,512]{1,0:T(8,128)(2,1)}, bf16[384,512]{1,0:T(8,128)(2,1)}, u32[]{:S(2)}, u32[]{:S(2)}) collective-permute-start(bf16[384,512]{1,0:T(8,128)(2,1)} %get-tuple-element.107), channel_id=1, source_target_pairs={{4,0},{5,1},{8,4},{9,5},{12,8},{13,9},{14,12},{15,13},{10,14},{11,... | collective-permute-start | bytes 1179656 | tf_op jit(solution)/shard_map/ppermute | solution.py:459
  164.8 28.6 %collective-permute-start.5 = (bf16[2,2,384,512]{3,2,1,0:T(8,128)(2,1)}, bf16[2,2,384,512]{3,2,1,0:T(8,128)(2,1)}, u32[]{:S(2)}, u32[]{:S(2)}) collective-permute-start(bf16[2,2,384,512]{3,2,1,0:T(8,128)(2,1)} %get-tuple-element.70), channel_id=1, source_target_pairs={{0,1},{1,0},{2,3},{3,2},{4,5},{5,4},{6,7},{7,6},{8,9},{9,8},{10,11... | collective-permute-start | bytes 4718600 | tf_op jit(solution)/shard_map/ppermute | solution.py:448
  164.8 57.8 %collective-permute-start.37 = (bf16[2,2,384,512]{3,2,1,0:T(8,128)(2,1)}, bf16[2,2,384,512]{3,2,1,0:T(8,128)(2,1)}, u32[]{:S(2)}, u32[]{:S(2)}) collective-permute-start(bf16[2,2,384,512]{3,2,1,0:T(8,128)(2,1)} %get-tuple-element.103), channel_id=1, source_target_pairs={{0,1},{1,0},{2,3},{3,2},{4,5},{5,4},{6,7},{7,6},{8,9},{9,8},{10,11... | collective-permute-start | bytes 4718600 | tf_op jit(solution)/shard_map/ppermute | solution.py:448
  165.3 21.1 %collective-permute-start.14 = (bf16[384,512]{1,0:T(8,128)(2,1)}, bf16[384,512]{1,0:T(8,128)(2,1)}, u32[]{:S(2)}, u32[]{:S(2)}) collective-permute-start(bf16[384,512]{1,0:T(8,128)(2,1)} %get-tuple-element.82), channel_id=1, source_target_pairs={{4,0},{5,1},{8,4},{9,5},{12,8},{13,9},{14,12},{15,13},{10,14},{11,... | collective-permute-start | bytes 1179656 | tf_op jit(solution)/shard_map/ppermute | solution.py:459
  168.3 20.6 %collective-permute-start.41 = (bf16[384,512]{1,0:T(8,128)(2,1)}, bf16[384,512]{1,0:T(8,128)(2,1)}, u32[]{:S(2)}, u32[]{:S(2)}) collective-permute-start(bf16[384,512]{1,0:T(8,128)(2,1)} %get-tuple-element.108), channel_id=1, source_target_pairs={{0,4},{1,5},{4,8},{5,9},{8,12},{9,13},{12,14},{13,15},{14,10},{15,... | collective-permute-start | bytes 1179656 | tf_op jit(solution)/shard_map/ppermute | solution.py:458
  169.8 20.6 %collective-permute-start.42 = (bf16[384,512]{1,0:T(8,128)(2,1)}, bf16[384,512]{1,0:T(8,128)(2,1)}, u32[]{:S(2)}, u32[]{:S(2)}) collective-permute-start(bf16[384,512]{1,0:T(8,128)(2,1)} %get-tuple-element.109), channel_id=1, source_target_pairs={{4,0},{5,1},{8,4},{9,5},{12,8},{13,9},{14,12},{15,13},{10,14},{11,... | collective-permute-start | bytes 1179656 | tf_op jit(solution)/shard_map/ppermute | solution.py:459
  186.4 46.2 %collective-permute-start.4 = (bf16[2,2,384,512]{3,2,1,0:T(8,128)(2,1)}, bf16[2,2,384,512]{3,2,1,0:T(8,128)(2,1)}, u32[]{:S(2)}, u32[]{:S(2)}) collective-permute-start(bf16[2,2,384,512]{3,2,1,0:T(8,128)(2,1)} %get-tuple-element.68), channel_id=1, source_target_pairs={{0,1},{1,0},{2,3},{3,2},{4,5},{5,4},{6,7},{7,6},{8,9},{9,8},{10,11... | collective-permute-start | bytes 4718600 | tf_op jit(solution)/shard_map/ppermute | solution.py:448
  188.9 12.3 %collective-permute-start.15 = (bf16[384,512]{1,0:T(8,128)(2,1)}, bf16[384,512]{1,0:T(8,128)(2,1)}, u32[]{:S(2)}, u32[]{:S(2)}) collective-permute-start(bf16[384,512]{1,0:T(8,128)(2,1)} %get-tuple-element.83), channel_id=1, source_target_pairs={{0,4},{1,5},{4,8},{5,9},{8,12},{9,13},{12,14},{13,15},{14,10},{15,... | collective-permute-start | bytes 1179656 | tf_op jit(solution)/shard_map/ppermute | solution.py:458
  193.4 16.3 %collective-permute-start.43 = (bf16[384,512]{1,0:T(8,128)(2,1)}, bf16[384,512]{1,0:T(8,128)(2,1)}, u32[]{:S(2)}, u32[]{:S(2)}) collective-permute-start(bf16[384,512]{1,0:T(8,128)(2,1)} %get-tuple-element.110), channel_id=1, source_target_pairs={{0,4},{1,5},{4,8},{5,9},{8,12},{9,13},{12,14},{13,15},{14,10},{15,... | collective-permute-start | bytes 1179656 | tf_op jit(solution)/shard_map/ppermute | solution.py:458
  204.9 13.2 %collective-permute-start.17 = (bf16[384,512]{1,0:T(8,128)(2,1)}, bf16[384,512]{1,0:T(8,128)(2,1)}, u32[]{:S(2)}, u32[]{:S(2)}) collective-permute-start(bf16[384,512]{1,0:T(8,128)(2,1)} %get-tuple-element.85), channel_id=1, source_target_pairs={{0,4},{1,5},{4,8},{5,9},{8,12},{9,13},{12,14},{13,15},{14,10},{15,... | collective-permute-start | bytes 1179656 | tf_op jit(solution)/shard_map/ppermute | solution.py:458
  220.2 75.3 %collective-permute-start.36 = (bf16[2,2,384,512]{3,2,1,0:T(8,128)(2,1)}, bf16[2,2,384,512]{3,2,1,0:T(8,128)(2,1)}, u32[]{:S(2)}, u32[]{:S(2)}) collective-permute-start(bf16[2,2,384,512]{3,2,1,0:T(8,128)(2,1)} %get-tuple-element.101), channel_id=1, source_target_pairs={{0,1},{1,0},{2,3},{3,2},{4,5},{5,4},{6,7},{7,6},{8,9},{9,8},{10,11... | collective-permute-start | bytes 4718600 | tf_op jit(solution)/shard_map/ppermute | solution.py:448
  222.6 13.3 %collective-permute-start.19 = (bf16[384,512]{1,0:T(8,128)(2,1)}, bf16[384,512]{1,0:T(8,128)(2,1)}, u32[]{:S(2)}, u32[]{:S(2)}) collective-permute-start(bf16[384,512]{1,0:T(8,128)(2,1)} %get-tuple-element.87), channel_id=1, source_target_pairs={{0,4},{1,5},{4,8},{5,9},{8,12},{9,13},{12,14},{13,15},{14,10},{15,... | collective-permute-start | bytes 1179656 | tf_op jit(solution)/shard_map/ppermute | solution.py:458
  226.1 12.3 %collective-permute-start.20 = (bf16[384,512]{1,0:T(8,128)(2,1)}, bf16[384,512]{1,0:T(8,128)(2,1)}, u32[]{:S(2)}, u32[]{:S(2)}) collective-permute-start(bf16[384,512]{1,0:T(8,128)(2,1)} %get-tuple-element.88), channel_id=1, source_target_pairs={{4,0},{5,1},{8,4},{9,5},{12,8},{13,9},{14,12},{15,13},{10,14},{11,... | collective-permute-start | bytes 1179656 | tf_op jit(solution)/shard_map/ppermute | solution.py:459
  232.6 14.1 %collective-permute-start.48 = (bf16[384,512]{1,0:T(8,128)(2,1)}, bf16[384,512]{1,0:T(8,128)(2,1)}, u32[]{:S(2)}, u32[]{:S(2)}) collective-permute-start(bf16[384,512]{1,0:T(8,128)(2,1)} %get-tuple-element.115), channel_id=1, source_target_pairs={{4,0},{5,1},{8,4},{9,5},{12,8},{13,9},{14,12},{15,13},{10,14},{11,... | collective-permute-start | bytes 1179656 | tf_op jit(solution)/shard_map/ppermute | solution.py:459
  235.9 54.9 %collective-permute-start.24 = (bf16[512,768]{1,0:T(8,128)(2,1)}, bf16[512,768]{1,0:T(8,128)(2,1)}, u32[]{:S(2)}, u32[]{:S(2)}) collective-permute-start(bf16[512,768]{1,0:T(8,128)(2,1)} %constant_dynamic-slice_fusion), channel_id=1, source_target_pairs={{0,1},{1,3},{2,5},{3,7},{4,9},{5,11},{6,13},{7,15},{8,17},{9,19},{... | collective-permute-start | bytes 2359304 | tf_op jit(solution)/shard_map/ppermute | solution.py:425
  238.4 52.4 %collective-permute-start.23 = (bf16[512,768]{1,0:T(8,128)(2,1)}, bf16[512,768]{1,0:T(8,128)(2,1)}, u32[]{:S(2)}, u32[]{:S(2)}) collective-permute-start(bf16[512,768]{1,0:T(8,128)(2,1)} %constant_dynamic-slice_fusion.1), channel_id=1, source_target_pairs={{0,1},{1,3},{2,5},{3,7},{4,9},{5,11},{6,13},{7,15},{8,17},{9,19},{... | collective-permute-start | bytes 2359304 | tf_op jit(solution)/shard_map/ppermute | solution.py:425
  246.7 41.5 %collective-permute-start.22 = (bf16[384,512]{1,0:T(8,128)(2,1)}, bf16[384,512]{1,0:T(8,128)(2,1)}, u32[]{:S(2)}, u32[]{:S(2)}) collective-permute-start(bf16[384,512]{1,0:T(8,128)(2,1)} %get-tuple-element.90), channel_id=1, source_target_pairs={{4,0},{5,1},{8,4},{9,5},{12,8},{13,9},{14,12},{15,13},{10,14},{11,... | collective-permute-start | bytes 1179656 | tf_op jit(solution)/shard_map/ppermute | solution.py:459
  253.2 42.3 %collective-permute-start.49 = (bf16[384,512]{1,0:T(8,128)(2,1)}, bf16[384,512]{1,0:T(8,128)(2,1)}, u32[]{:S(2)}, u32[]{:S(2)}) collective-permute-start(bf16[384,512]{1,0:T(8,128)(2,1)} %get-tuple-element.116), channel_id=1, source_target_pairs={{0,4},{1,5},{4,8},{5,9},{8,12},{9,13},{12,14},{13,15},{14,10},{15,... | collective-permute-start | bytes 1179656 | tf_op jit(solution)/shard_map/ppermute | solution.py:458
  301.6 21.4 %collective-permute-start.51 = (bf16[384,512]{1,0:T(8,128)(2,1)}, bf16[384,512]{1,0:T(8,128)(2,1)}, u32[]{:S(2)}, u32[]{:S(2)}) collective-permute-start(bf16[384,512]{1,0:T(8,128)(2,1)} %get-tuple-element.118), channel_id=1, source_target_pairs={{0,4},{1,5},{4,8},{5,9},{8,12},{9,13},{12,14},{13,15},{14,10},{15,... | collective-permute-start | bytes 1179656 | tf_op jit(solution)/shard_map/ppermute | solution.py:458
  301.6 21.4 %collective-permute-start.52 = (bf16[384,512]{1,0:T(8,128)(2,1)}, bf16[384,512]{1,0:T(8,128)(2,1)}, u32[]{:S(2)}, u32[]{:S(2)}) collective-permute-start(bf16[384,512]{1,0:T(8,128)(2,1)} %get-tuple-element.119), channel_id=1, source_target_pairs={{4,0},{5,1},{8,4},{9,5},{12,8},{13,9},{14,12},{15,13},{10,14},{11,... | collective-permute-start | bytes 1179656 | tf_op jit(solution)/shard_map/ppermute | solution.py:459
  329.2 14.9 %collective-permute-start.53 = (bf16[256,512]{1,0:T(8,128)(2,1)}, bf16[256,512]{1,0:T(8,128)(2,1)}, u32[]{:S(2)}, u32[]{:S(2)}) collective-permute-start(bf16[256,512]{1,0:T(8,128)(2,1)} %get-tuple-element.123), channel_id=1, source_target_pairs={{0,1},{1,0},{2,3},{3,2},{4,5},{5,4},{6,7},{7,6},{8,9},{9,8},{10,11... | collective-permute-start | bytes 786440 | tf_op jit(solution)/shard_map/ppermute | solution.py:131
  344.0 32.2 %collective-permute-start.35 = (bf16[512,512]{1,0:T(8,128)(2,1)}, bf16[512,512]{1,0:T(8,128)(2,1)}, u32[]{:S(2)}, u32[]{:S(2)}) collective-permute-start(bf16[512,512]{1,0:T(8,128)(2,1)} %place.2.low_ref), channel_id=1, source_target_pairs={{0,1},{1,0},{2,3},{3,2},{4,5},{5,4},{6,7},{7,6},{8,9},{9,8},{10,11... | collective-permute-start | bytes 1572872 | tf_op jit(solution)/shard_map/ppermute | solution.py:131
  (36 other events, 336.2 us)
